TPU v7x, 32 devices: a whole 2x2x4 slice. The times are simulated.
32 devices in a mesh: dp: 8 (over y, x, core), tensor: 4 (over z).
Axes of the slice: x: 2, y: 2, z: 4, core: 2. Of those that a mesh axis runs over, the one named last changes fastest.
Arguments:
- inputs: bfloat16 [16, 1024, 1024], P('dp', 'tensor'), may hold values from -6 to 6
- cotangent: bfloat16 [16, 1024, 1024], P('dp', 'tensor'), may hold values from -6 to 6
- lengths: int32 [16], P('dp'), may hold values from 1 to 1024, as said below
- block_ids: int32 [16, 1024], P('dp'), may hold values from 0 to 7, never falling along the last dimension, each value on 1 to 256 neighbouring positions
- ln1_gain: float32 [1024], replicated, may hold values from 0.5 to 1.5
- ln1_bias: float32 [1024], replicated, may hold values from -1 to 1
- ln2_gain: float32 [1024], replicated, may hold values from 0.5 to 1.5
- ln2_bias: float32 [1024], replicated, may hold values from -1 to 1
- w_qkv: bfloat16 [1024, 3072], P('dp', 'tensor'), may hold values from -0.1875 to 0.1875
- b_qkv: float32 [3072], P('tensor'), may hold values from -1 to 1
- w_out: bfloat16 [1024, 1024], P('dp', 'tensor'), may hold values from -1 to 1
- b_out: float32 [1024], replicated, may hold values from -1 to 1
- w_up: bfloat16 [1024, 4096], P('dp', 'tensor'), may hold values from -0.1875 to 0.1875
- b_up: float32 [4096], P('tensor'), may hold values from -1 to 1
- w_down: bfloat16 [1024, 4096], P('dp', 'tensor'), may hold values from -0.09375 to 0.09375
- b_down: float32 [1024], replicated, may hold values from -1 to 1
Outputs:
- layer_out: bfloat16 [16, 1024, 1024], P('dp', 'tensor')
- grad_inputs: float32 [16, 1024, 1024], P('dp', 'tensor')
- grad_w_qkv: float32 [1024, 3072], P('dp', 'tensor')
- grad_w_out: float32 [1024, 1024], P('dp', 'tensor')
- grad_w_up: float32 [1024, 4096], P('dp', 'tensor')
- grad_w_down: float32 [1024, 4096], P('dp', 'tensor')
- grad_b_qkv: float32 [3072], P('tensor')
- grad_b_up: float32 [4096], P('tensor')
- grad_ln1_gain: float32 [1024], replicated
- grad_ln1_bias: float32 [1024], replicated
- grad_ln2_gain: float32 [1024], replicated
- grad_ln2_bias: float32 [1024], replicated
- grad_b_out: float32 [1024], replicated
- grad_b_down: float32 [1024], replicated
Inputs may be any that keep to these rules, and one draw needn't show every extreme that they name: `lengths`: live tokens of each sequence, at its start; keys from the length on are padding; some sequence has all 1024 live. `block_ids`: along each sequence the block number starts at 0 and never falls; each block spans 1 to 256 consecutive positions and some block spans exactly 256.
All inputs are finite; a program needn't handle non-finite values.
Results may differ from a plain program's by a relative error of at most 0.0098.
Values may be sent and summed in bfloat16 or wider, within the bound.
A program may use at most 256 MiB of HBM per device.

v0:
```python
import jax
import jax.numpy as jnp
from jax import lax
from jax.sharding import PartitionSpec as P

HEAD = 64
ROT = 16
BLOCK = 256
MICRO = 2


def layer_norm(values, ln_gain, ln_bias):
    centre = jnp.mean(values, axis=-1, keepdims=True)
    shifted = values - centre
    spread = jnp.mean(shifted * shifted, axis=-1, keepdims=True)
    return shifted * lax.rsqrt(spread + 1e-05) * ln_gain + ln_bias


def rope_tables(length, rotary):
    halved = rotary // 2
    frequency = 1.0 / 10000.0 ** (jnp.arange(halved, dtype=jnp.float32) * (2.0 / rotary))
    angles = jnp.arange(length, dtype=jnp.float32)[:, None] * frequency[None, :]
    angles = jnp.concatenate([angles, angles], axis=1)[:, None, :]
    return (jnp.cos(angles), jnp.sin(angles))


def rotate(head_rows, cos_table, sin_table, rotary):
    halved = rotary // 2
    moving = head_rows[..., :rotary]
    turned = jnp.concatenate([-moving[..., halved:], moving[..., :halved]], axis=-1)
    moving = moving * cos_table + turned * sin_table
    return jnp.concatenate([moving, head_rows[..., rotary:]], axis=-1)


def visible(block_rows, limits, first_row, tile_rows, key_end):
    own_ids = block_rows[:, first_row : first_row + tile_rows]
    key_pos = jnp.arange(key_end, dtype=jnp.int32)
    allowed = (block_rows[:, None, :key_end] <= own_ids[:, :, None]) & (
        key_pos[None, None, :] < limits[:, None, None]
    )
    return allowed[:, None]


def gelu_exact(argument):
    return jax.nn.gelu(argument, approximate=False)


def on_device(
    inputs,
    cotangent,
    lengths,
    block_ids,
    ln1_gain,
    ln1_bias,
    ln2_gain,
    ln2_bias,
    w_qkv,
    b_qkv,
    w_out,
    b_out,
    w_up,
    b_up,
    w_down,
    b_down,
):
    model_width = inputs.shape[2]
    per_micro = inputs.shape[0] // MICRO
    length = block_ids.shape[1]
    tile_rows = min(512, length)
    heads_here = w_qkv.shape[1] // (3 * HEAD)
    scaling = HEAD ** (-0.5)
    cos_table, sin_table = rope_tables(length, ROT)
    grad_qkv = jnp.zeros((model_width, w_qkv.shape[1]), jnp.float32)
    grad_outw = jnp.zeros((model_width, w_out.shape[1]), jnp.float32)
    grad_upw = jnp.zeros((model_width, w_up.shape[1]), jnp.float32)
    grad_downw = jnp.zeros((model_width, w_down.shape[1]), jnp.float32)
    sum_bias_qkv = jnp.zeros((w_qkv.shape[1],), jnp.float32)
    sum_bias_up = jnp.zeros((w_up.shape[1],), jnp.float32)
    sum_gain_one = jnp.zeros((model_width,), jnp.float32)
    sum_bias_one = jnp.zeros((model_width,), jnp.float32)
    sum_gain_two = jnp.zeros((model_width,), jnp.float32)
    sum_bias_two = jnp.zeros((model_width,), jnp.float32)
    sum_slope = jnp.zeros((model_width,), jnp.float32)
    out_rows = []
    grad_rows = []
    tile_starts = list(range(0, length, tile_rows))
    key_ends = [min(length, first_row + tile_rows + BLOCK) for first_row in tile_starts]
    for micro_idx in range(MICRO):
        first_seq = micro_idx * per_micro
        last_seq = first_seq + per_micro
        residual = inputs[first_seq:last_seq].astype(jnp.float32)
        limits = lengths[first_seq:last_seq]
        block_rows = block_ids[first_seq:last_seq]
        value_one, norm_one_back = jax.vjp(layer_norm, residual, ln1_gain, ln1_bias)
        value_two, norm_two_back = jax.vjp(layer_norm, residual, ln2_gain, ln2_bias)
        whole_one, whole_two = (
            lax.all_gather(value_one.astype(jnp.bfloat16), "tensor", axis=1, tiled=True),
            lax.all_gather(value_two.astype(jnp.bfloat16), "tensor", axis=1, tiled=True),
        )
        qkv_full, out_full, up_full, down_full = (
            lax.all_gather(w_qkv, "dp", axis=0, tiled=True),
            lax.all_gather(w_out, "dp", axis=0, tiled=True),
            lax.all_gather(w_up, "dp", axis=0, tiled=True),
            lax.all_gather(w_down, "dp", axis=0, tiled=True),
        )
        projected = (
            jnp.einsum("bsd,dc->bsc", whole_one, qkv_full, preferred_element_type=jnp.float32)
            + b_qkv
        )
        projected = projected.reshape(per_micro, length, heads_here, 3, HEAD)
        queries = rotate(projected[:, :, :, 0], cos_table, sin_table, ROT).astype(jnp.bfloat16)
        key_rows = rotate(projected[:, :, :, 1], cos_table, sin_table, ROT).astype(jnp.bfloat16)
        values = projected[:, :, :, 2].astype(jnp.bfloat16)
        scaled_q = (queries * jnp.bfloat16(scaling)).transpose(0, 2, 1, 3)
        keys_hd = key_rows.transpose(0, 2, 1, 3)
        values_hd = values.transpose(0, 2, 1, 3)
        log_sums = []
        mixed_parts = []
        for first_row, key_end in zip(tile_starts, key_ends):
            q_block = scaled_q[:, :, first_row : first_row + tile_rows]
            allowed = visible(block_rows, limits, first_row, tile_rows, key_end)
            scores = jnp.einsum(
                "bhqe,bhke->bhqk",
                q_block,
                keys_hd[:, :, :key_end],
                preferred_element_type=jnp.float32,
            )
            scores = jnp.where(allowed, scores, -1e30)
            row_peak = jnp.max(scores, axis=-1)
            powered = jnp.exp(scores - row_peak[..., None])
            totals = jnp.sum(powered, axis=-1)
            soft_low = (powered / totals[..., None]).astype(jnp.bfloat16)
            log_sums.append(row_peak + jnp.log(totals))
            mixed_parts.append(
                jnp.einsum(
                    "bhqk,bhke->bhqe",
                    soft_low,
                    values_hd[:, :, :key_end],
                    preferred_element_type=jnp.float32,
                )
            )
        attended = (
            jnp.concatenate(mixed_parts, axis=2)
            .transpose(0, 2, 1, 3)
            .reshape(per_micro, length, heads_here * HEAD)
            .astype(jnp.bfloat16)
        )
        partial_sum = jnp.einsum(
            "bsf,df->bsd", attended, out_full, preferred_element_type=jnp.float32
        )
        hidden_pre = (
            jnp.einsum("bsd,df->bsf", whole_two, up_full, preferred_element_type=jnp.float32) + b_up
        )
        gelu_value, gelu_back = jax.vjp(gelu_exact, hidden_pre)
        activated = gelu_value.astype(jnp.bfloat16)
        partial_sum = partial_sum + jnp.einsum(
            "bsf,df->bsd", activated, down_full, preferred_element_type=jnp.float32
        )
        reduced = lax.psum_scatter(partial_sum, "tensor", scatter_dimension=1, tiled=True)
        out_rows.append((residual + reduced + b_out + b_down).astype(jnp.bfloat16))
        slope_local = cotangent[first_seq:last_seq]
        slope = lax.all_gather(slope_local, "tensor", axis=1, tiled=True)
        qkv_full, out_full, up_full, down_full = (
            lax.all_gather(w_qkv, "dp", axis=0, tiled=True),
            lax.all_gather(w_out, "dp", axis=0, tiled=True),
            lax.all_gather(w_up, "dp", axis=0, tiled=True),
            lax.all_gather(w_down, "dp", axis=0, tiled=True),
        )
        grad_outw = grad_outw + jnp.einsum(
            "bsd,bsf->df", slope, attended, preferred_element_type=jnp.float32
        )
        grad_downw = grad_downw + jnp.einsum(
            "bsd,bsf->df", slope, activated, preferred_element_type=jnp.float32
        )
        grad_att = jnp.einsum(
            "bsd,df->bsf", slope, out_full, preferred_element_type=jnp.float32
        ).astype(jnp.bfloat16)
        grad_att = grad_att.reshape(per_micro, length, heads_here, HEAD).transpose(0, 2, 1, 3)
        grad_act = jnp.einsum("bsd,df->bsf", slope, down_full, preferred_element_type=jnp.float32)
        grad_hidden = gelu_back(grad_act)[0].astype(jnp.bfloat16)
        grad_upw = grad_upw + jnp.einsum(
            "bsd,bsf->df", whole_two, grad_hidden, preferred_element_type=jnp.float32
        )
        sum_bias_up = sum_bias_up + jnp.sum(grad_hidden.astype(jnp.float32), axis=(0, 1))
        grad_two = jnp.einsum(
            "bsf,df->bsd", grad_hidden, up_full, preferred_element_type=jnp.float32
        )
        grad_keys = jnp.zeros((per_micro, heads_here, length, HEAD), jnp.float32)
        grad_values = jnp.zeros((per_micro, heads_here, length, HEAD), jnp.float32)
        query_parts = []
        for index_tile, first_row in enumerate(tile_starts):
            key_end = key_ends[index_tile]
            q_block = scaled_q[:, :, first_row : first_row + tile_rows]
            g_block = grad_att[:, :, first_row : first_row + tile_rows]
            k_block = keys_hd[:, :, :key_end]
            allowed = visible(block_rows, limits, first_row, tile_rows, key_end)
            scores = jnp.einsum(
                "bhqe,bhke->bhqk", q_block, k_block, preferred_element_type=jnp.float32
            )
            scores = jnp.where(allowed, scores, -1e30)
            soft_full = jnp.exp(scores - log_sums[index_tile][..., None])
            soft_low = soft_full.astype(jnp.bfloat16)
            value_part = jnp.einsum(
                "bhqk,bhqe->bhke", soft_low, g_block, preferred_element_type=jnp.float32
            )
            grad_values = grad_values.at[:, :, :key_end].add(value_part)
            grad_soft = jnp.einsum(
                "bhqe,bhke->bhqk",
                g_block,
                values_hd[:, :, :key_end],
                preferred_element_type=jnp.float32,
            )
            centred = jnp.sum(soft_full * grad_soft, axis=-1)
            grad_scores = (soft_full * (grad_soft - centred[..., None])).astype(jnp.bfloat16)
            query_parts.append(
                jnp.einsum(
                    "bhqk,bhke->bhqe", grad_scores, k_block, preferred_element_type=jnp.float32
                )
                * scaling
            )
            key_part = jnp.einsum(
                "bhqk,bhqe->bhke", grad_scores, q_block, preferred_element_type=jnp.float32
            )
            grad_keys = grad_keys.at[:, :, :key_end].add(key_part)
        grad_queries = jnp.concatenate(query_parts, axis=2).transpose(0, 2, 1, 3)
        grad_keys = grad_keys.transpose(0, 2, 1, 3)
        grad_values = grad_values.transpose(0, 2, 1, 3)
        grad_projected = jnp.stack(
            [
                rotate(grad_queries, cos_table, -sin_table, ROT),
                rotate(grad_keys, cos_table, -sin_table, ROT),
                grad_values,
            ],
            axis=3,
        )
        grad_projected = grad_projected.reshape(per_micro, length, 3 * heads_here * HEAD).astype(
            jnp.bfloat16
        )
        grad_qkv = grad_qkv + jnp.einsum(
            "bsd,bsc->dc", whole_one, grad_projected, preferred_element_type=jnp.float32
        )
        sum_bias_qkv = sum_bias_qkv + jnp.sum(grad_projected.astype(jnp.float32), axis=(0, 1))
        grad_one = jnp.einsum(
            "bsc,dc->bsd", grad_projected, qkv_full, preferred_element_type=jnp.float32
        )
        slope_rows = slope_local.astype(jnp.float32)
        back_one, back_two = (
            lax.psum_scatter(grad_one, "tensor", scatter_dimension=1, tiled=True),
            lax.psum_scatter(grad_two, "tensor", scatter_dimension=1, tiled=True),
        )
        input_one, gain_one, bias_one = norm_one_back(back_one)
        input_two, gain_two, bias_two = norm_two_back(back_two)
        grad_rows.append(slope_rows + input_one + input_two)
        sum_gain_one = sum_gain_one + gain_one
        sum_bias_one = sum_bias_one + bias_one
        sum_gain_two = sum_gain_two + gain_two
        sum_bias_two = sum_bias_two + bias_two
        sum_slope = sum_slope + jnp.sum(slope_rows, axis=(0, 1))
    reduced_grads = (
        lax.psum_scatter(grad_qkv, "dp", scatter_dimension=0, tiled=True),
        lax.psum_scatter(grad_outw, "dp", scatter_dimension=0, tiled=True),
        lax.psum_scatter(grad_upw, "dp", scatter_dimension=0, tiled=True),
        lax.psum_scatter(grad_downw, "dp", scatter_dimension=0, tiled=True),
    )
    bias_qkv_total, bias_up_total = lax.psum((sum_bias_qkv, sum_bias_up), "dp")
    shared = lax.psum(
        (sum_gain_one, sum_bias_one, sum_gain_two, sum_bias_two, sum_slope), ("dp", "tensor")
    )
    return (
        jnp.concatenate(out_rows, axis=0),
        jnp.concatenate(grad_rows, axis=0),
        reduced_grads[0],
        reduced_grads[1],
        reduced_grads[2],
        reduced_grads[3],
        bias_qkv_total,
        bias_up_total,
        shared[0],
        shared[1],
        shared[2],
        shared[3],
        shared[4],
        shared[4],
    )


def solution(mesh):
    in_specs = (
        P("dp", "tensor", None),
        P("dp", "tensor", None),
        P("dp"),
        P("dp", None),
        P(),
        P(),
        P(),
        P(),
        P("dp", "tensor"),
        P("tensor"),
        P("dp", "tensor"),
        P(),
        P("dp", "tensor"),
        P("tensor"),
        P("dp", "tensor"),
        P(),
    )
    out_specs = (
        P("dp", "tensor", None),
        P("dp", "tensor", None),
        P("dp", "tensor"),
        P("dp", "tensor"),
        P("dp", "tensor"),
        P("dp", "tensor"),
        P("tensor"),
        P("tensor"),
        P(),
        P(),
        P(),
        P(),
        P(),
        P(),
    )
    return jax.shard_map(
        on_device, mesh=mesh, in_specs=in_specs, out_specs=out_specs, check_vma=False
    )
```

profile of v0, /device:TPU:0, one launch (start us, length us, event | category | flops | bytes accessed | tf_op | source)
XLA Modules:
  0.0 1063.5 jit_solution(9621609152329100266)
XLA Ops:
  11.7 3.2 fusion.173
  24.5 12.7 %all_gather.44 = bf16[1024,256]{1,0:T(8,128)(2,1)S(1)} all-gather(bf16[128,256]{1,0:T(8,128)(2,1)S(1)} %copy-done.88), channel_id=1, replica_groups=mesh['dp'=8,'tensor'=4] {'dp'}, dimensions={0}, use_global_device_ids=true | all-gather | bytes 589824 | tf_op jit(solution)/shard_map/all_gather | solution.py:102
  39.7 48.1 %all-gather.10.cloned.1.call-done = bf16[1,1024,1024]{2,1,0:T(8,128)(2,1)} async-done(((bf16[1,256,1024]{2,1,0:T(8,128)(2,1)}), bf16[1,1024,1024]{2,1,0:T(8,128)(2,1)}) %all-gather.10.cloned.1.call-update) | async-done | bytes 2097168 | tf_op jit(solution)/shard_map/all_gather | solution.py:97
  87.8 3.9 fusion.85
  96.9 37.2 %all-gather.20.cloned.1.call-done = bf16[1,1024,1024]{2,1,0:T(8,128)(2,1)} async-done(((bf16[1,256,1024]{2,1,0:T(8,128)(2,1)}), bf16[1,1024,1024]{2,1,0:T(8,128)(2,1)}) %all-gather.20.cloned.1.call-update) | async-done | bytes 2097168 | tf_op jit(solution)/shard_map/all_gather | solution.py:97
  134.1 3.9 fusion.91
  147.8 2.8 fusion.161
  150.5 29.7 %all-gather.24.cloned.1.call-done = bf16[1,1024,1024]{2,1,0:T(8,128)(2,1)} async-done(((bf16[1,256,1024]{2,1,0:T(8,128)(2,1)}), bf16[1,1024,1024]{2,1,0:T(8,128)(2,1)}) %all-gather.24.cloned.1.call-update) | async-done | bytes 2097168 | tf_op jit(solution)/shard_map/all_gather | solution.py:162
  180.2 2.3 fusion.142
  182.6 4.8 multiply_reduce_fusion.3
  194.4 2.2 fusion
  197.7 3.6 fusion.155
  202.8 2.1 fusion.3
  205.0 2.0 fusion.160
  208.6 2.3 fusion.1
  212.0 3.8 fusion.154
  215.9 10.4 all-gather.26.cloned.1.call-done
  226.3 3.3 fusion.145
  229.6 2.4 fusion.46
  234.4 6.3 multiply_reduce_fusion.1
  240.8 2.3 multiply_convert_fusion.1
  243.2 2.2 fusion.158
  247.4 2.6 multiply_reduce_fusion.2
  251.7 21.3 %all-gather.22.cloned.1.call-done = bf16[1,1024,1024]{2,1,0:T(8,128)(2,1)} async-done(((bf16[1,256,1024]{2,1,0:T(8,128)(2,1)}), bf16[1,1024,1024]{2,1,0:T(8,128)(2,1)}) %all-gather.22.cloned.1.call-update) | async-done | bytes 2097168 | tf_op jit(solution)/shard_map/all_gather | solution.py:98
  273.0 28.5 %all-gather.16.cloned.1.call-done = bf16[1024,1024]{1,0:T(8,128)(2,1)} async-done(((bf16[128,1024]{1,0:T(8,128)(2,1)}), bf16[1024,1024]{1,0:T(8,128)(2,1)}) %all-gather.16.cloned.1.call-update) | async-done | bytes 2097168 | tf_op jit(solution)/shard_map/all_gather | solution.py:103
  301.5 6.6 fusion.66
  308.2 41.5 %all-gather.14.cloned.1.call-done = bf16[1,1024,1024]{2,1,0:T(8,128)(2,1)} async-done(((bf16[1,256,1024]{2,1,0:T(8,128)(2,1)}), bf16[1,1024,1024]{2,1,0:T(8,128)(2,1)}) %all-gather.14.cloned.1.call-update) | async-done | bytes 2097168 | tf_op jit(solution)/shard_map/all_gather | solution.py:98
  349.6 23.9 %multiply_convert_fusion.5 = (bf16[1024,1024]{1,0:T(8,128)(2,1)S(1)}, f32[1024,1024]{1,0:T(8,128)}, bf16[1024,1024]{1,0:T(8,128)(2,1)S(1)}, f32[1024,1024]{1,0:T(8,128)}, f32[1024,1024]{1,0:T(8,128)}) fusion(f32[1024]{0:T(1024)} %param.53, f32[1024,1024]{1,0:T(8,128)} %fusion.66, bf16[1024,1024]{1,0:T(8,128)(2,1)} %all-gather.16.cloned.1.call-done, ...), kind=kOutput, calls=%fused_computation.58 | convolution fusion | flops 2285895680 | bytes 25169920 | tf_op jit(solution)/shard_map/bsd,df->bsf/dot_general | solution.py:152
  373.6 2.4 fusion.44
  376.7 4.5 add_bitcast_fusion
  385.4 3.0 fusion.156
  388.4 6.6 multiply_reduce_fusion
  395.1 2.1 multiply_convert_fusion
  405.4 2.2 fusion.139
  409.1 3.9 convolution_bitcast_fusion.1
  414.7 4.4 fusion.151
  419.1 4.7 fusion.133
  425.5 3.9 convolution_bitcast_fusion
  431.1 7.4 convert_reduce_fusion
  439.9 4.4 convolution_bitcast_fusion.2
  445.9 6.8 convert_reduce_fusion.1
  454.2 4.5 convolution_bitcast_fusion.3
  460.2 4.0 fusion.252
  464.2 2.7 add_bitcast_fusion.1
  467.0 4.1 fusion.251
  471.1 2.8 add_bitcast_fusion.2
  475.3 3.6 fusion.68
  478.9 3.6 fusion.88
  482.6 4.8 fusion.64
  487.4 4.5 fusion.80
  492.2 16.0 %all-reduce.5 = (f32[768]{0:T(1024)}, f32[1024]{0:T(1024)}) all-reduce(f32[768]{0:T(1024)S(1)} %add.401, f32[1024]{0:T(1024)S(1)} %add.402), channel_id=1, replica_groups=mesh['dp'=8,'tensor'=4] {'dp'}, use_global_device_ids=true, to_apply=%region_36.37 | all-reduce | flops 1792 | bytes 14336 | tf_op jit(solution)/shard_map/psum | solution.py:265
  509.8 2.0 copy.58
  511.8 39.2 %reduce-scatter.15.cloned.1.call-done = f32[1,256,1024]{2,1,0:T(8,128)} async-done(((f32[1,1024,1024]{2,1,0:T(8,128)}), f32[1,256,1024]{2,1,0:T(8,128)}) %reduce-scatter.15.cloned.1.call-update) | async-done | bytes 1048592 | tf_op jit(solution)/shard_map/reduce_scatter | solution.py:248
  551.1 79.6 %reduce-scatter.19.cloned.1.call-done = f32[1,256,1024]{2,1,0:T(8,128)} async-done(((f32[1,1024,1024]{2,1,0:T(8,128)}), f32[1,256,1024]{2,1,0:T(8,128)}) %reduce-scatter.19.cloned.1.call-update) | async-done | bytes 1048592 | tf_op jit(solution)/shard_map/reduce_scatter | solution.py:248
  630.6 2.0 fusion.177
  632.7 77.5 %reduce-scatter.21.cloned.1.call-done = f32[1,256,1024]{2,1,0:T(8,128)} async-done(((f32[1,1024,1024]{2,1,0:T(8,128)}), f32[1,256,1024]{2,1,0:T(8,128)}) %reduce-scatter.21.cloned.1.call-update) | async-done | bytes 1048592 | tf_op jit(solution)/shard_map/reduce_scatter | solution.py:249
  710.2 79.4 %reduce-scatter.17.cloned.1.call-done = f32[1,256,1024]{2,1,0:T(8,128)} async-done(((f32[1,1024,1024]{2,1,0:T(8,128)}), f32[1,256,1024]{2,1,0:T(8,128)}) %reduce-scatter.17.cloned.1.call-update) | async-done | bytes 1048592 | tf_op jit(solution)/shard_map/reduce_scatter | solution.py:249
  789.7 3.2 fusion.178
  795.8 44.0 %all-reduce.4 = (f32[1024]{0:T(1024)}, f32[1024]{0:T(1024)}, f32[1024]{0:T(1024)}, f32[1024]{0:T(1024)}, f32[1024]{0:T(1024)S(1)}) all-reduce(f32[1024]{0:T(1024)S(1)} %add.403, f32[1024]{0:T(1024)S(1)} %add.404, f32[1024]{0:T(1024)S(1)} %add.405, f32[1024]{0:T(1024)S(1)} %add.406, ...), channel_id=1, replica_groups=mesh['dp'=8,'tensor'=4] {'dp','tensor'}, use_global_device_ids=true, to_apply=%region_42.43 | all-reduce | flops 5120 | bytes 40960 | tf_op jit(solution)/shard_map/psum | solution.py:266
  839.8 30.5 %reduce-scatter.13.cloned.1.call-done = f32[1,256,1024]{2,1,0:T(8,128)} async-done(((f32[1,1024,1024]{2,1,0:T(8,128)}), f32[1,256,1024]{2,1,0:T(8,128)}) %reduce-scatter.13.cloned.1.call-update) | async-done | bytes 1048592 | tf_op jit(solution)/shard_map/reduce_scatter | solution.py:159
  870.2 79.4 %reduce-scatter.11.cloned.1.call-done = f32[1,256,1024]{2,1,0:T(8,128)} async-done(((f32[1,1024,1024]{2,1,0:T(8,128)}), f32[1,256,1024]{2,1,0:T(8,128)}) %reduce-scatter.11.cloned.1.call-update) | async-done | bytes 1048592 | tf_op jit(solution)/shard_map/reduce_scatter | solution.py:159
  949.6 2.7 fusion.181
  954.9 45.7 %reduce-scatter.23.cloned.1.call-done = f32[128,768]{1,0:T(8,128)} async-done(((f32[1024,768]{1,0:T(8,128)}), f32[128,768]{1,0:T(8,128)}) %reduce-scatter.23.cloned.1.call-update) | async-done | bytes 393232 | tf_op jit(solution)/shard_map/reduce_scatter | solution.py:260
  1000.6 55.3 %reduce-scatter.27.cloned.1.call-done = f32[128,1024]{1,0:T(8,128)} async-done(((f32[1024,1024]{1,0:T(8,128)}), f32[128,1024]{1,0:T(8,128)}) %reduce-scatter.27.cloned.1.call-update) | async-done | bytes 524304 | tf_op jit(solution)/shard_map/reduce_scatter | solution.py:262
  (415 shorter events, 83.8 us)
Async XLA Ops:
  7.2 8.5 copy-start.16
  7.2 32.6 %all-gather.12.cloned.1.call-start = ((), (), s32[]{:S(2)}) async-start(), calls=%async_computation.11 | async-start | bytes 1769472 | tf_op jit(solution)/shard_map/all_gather | solution.py:101
  7.9 79.9 %all-gather.10.cloned.1.call-start = ((), (), s32[]{:S(2)}) async-start(), calls=%async_computation.10 | async-start | bytes 2621440 | tf_op jit(solution)/shard_map/all_gather | solution.py:97
  9.4 5.4 copy-start.92
  11.6 8.6 copy-start.105
  11.7 11.8 %copy-start.89 = (s32[2,1024]{1,0:T(2,128)S(1)}, s32[2,1024]{1,0:T(2,128)}, u32[]{:S(2)}) copy-start(s32[2,1024]{1,0:T(2,128)} %param.43) | copy-start | bytes 24580
  11.7 12.8 %copy-start.88 = (bf16[128,256]{1,0:T(8,128)(2,1)S(1)}, bf16[128,256]{1,0:T(8,128)(2,1)}, u32[]{:S(2)}) copy-start(bf16[128,256]{1,0:T(8,128)(2,1)} %param.50) | copy-start | bytes 196612
  14.8 73.0 %copy-start.113 = (f32[768]{0:T(1024)S(1)}, f32[768]{0:T(1024)}, u32[]{:S(2)}) copy-start(f32[768]{0:T(1024)} %param.49) | copy-start | bytes 9220
  14.9 119.2 %all-gather.20.cloned.1.call-start = ((), (), s32[]{:S(2)}) async-start(), calls=%async_computation.16 | async-start | bytes 2621440 | tf_op jit(solution)/shard_map/all_gather | solution.py:97
  15.6 164.6 %all-gather.24.cloned.1.call-start = ((), (), s32[]{:S(2)}) async-start(), calls=%async_computation.19 | async-start | bytes 2621440 | tf_op jit(solution)/shard_map/all_gather | solution.py:162
  16.8 209.5 %all-gather.26.cloned.1.call-start = ((), (), s32[]{:S(2)}) async-start(), calls=%async_computation.22 | async-start | bytes 2621440 | tf_op jit(solution)/shard_map/all_gather | solution.py:162
  17.4 255.6 %all-gather.22.cloned.1.call-start = ((), (), s32[]{:S(2)}) async-start(), calls=%async_computation.17 | async-start | bytes 2621440 | tf_op jit(solution)/shard_map/all_gather | solution.py:98
  18.0 283.6 %all-gather.16.cloned.1.call-start = ((), (), s32[]{:S(2)}) async-start(), calls=%async_computation.13 | async-start | bytes 2359296 | tf_op jit(solution)/shard_map/all_gather | solution.py:103
  18.7 330.9 %all-gather.14.cloned.1.call-start = ((), (), s32[]{:S(2)}) async-start(), calls=%async_computation.12 | async-start | bytes 2621440 | tf_op jit(solution)/shard_map/all_gather | solution.py:98
  19.5 410.0 %all-gather.18.cloned.1.call-start = ((), (), s32[]{:S(2)}) async-start(), calls=%async_computation.14 | async-start | bytes 2359296 | tf_op jit(solution)/shard_map/all_gather | solution.py:104
  20.2 487.9 %reduce-scatter.25.cloned.1.call-start = ((), (), s32[]{:S(2)}) async-start(), calls=%async_computation.26 | async-start | bytes 1179648 | tf_op jit(solution)/shard_map/reduce_scatter | solution.py:261
  37.2 189.1 %copy-start.21 = (bf16[1024,256]{1,0:T(8,128)(2,1)}, bf16[1024,256]{1,0:T(8,128)(2,1)S(1)}, u32[]{:S(2)}) copy-start(bf16[1024,256]{1,0:T(8,128)(2,1)S(1)} %all_gather.44) | copy-start | bytes 1572868
  37.6 173.3 %copy-start.7 = (pred[512,1024]{1,0:T(8,128)(4,1)}, pred[512,1024]{1,0:T(8,128)(4,1)S(1)}, u32[]{:S(2)}) copy-start(pred[512,1024]{1,0:T(8,128)(4,1)S(1)} %compare_and_fusion) | copy-start | bytes 1572868
  38.0 202.7 %copy-start.10 = (pred[512,1024]{1,0:T(8,128)(4,1)}, pred[512,1024]{1,0:T(8,128)(4,1)S(1)}, u32[]{:S(2)}) copy-start(pred[512,1024]{1,0:T(8,128)(4,1)S(1)} %compare_and_fusion.1) | copy-start | bytes 1572868
  38.6 148.7 %copy-start.5 = (pred[512,768]{1,0:T(8,128)(4,1)}, pred[512,768]{1,0:T(8,128)(4,1)S(1)}, u32[]{:S(2)}) copy-start(pred[512,768]{1,0:T(8,128)(4,1)S(1)} %get-tuple-element.314) | copy-start | bytes 1179652
  143.6 49.2 %copy-start.60 = (bf16[1,1024,4,16]{1,3,2,0:T(8,128)(2,1)}, bf16[1,1024,4,16]{1,3,2,0:T(8,128)(2,1)S(1)}, u32[]{:S(2)}) copy-start(bf16[1,1024,4,16]{1,3,2,0:T(8,128)(2,1)S(1)} %get-tuple-element.271) | copy-start | bytes 393220
  143.6 63.4 %copy-start.58 = (bf16[1,1024,4,16]{1,3,2,0:T(8,128)(2,1)}, bf16[1,1024,4,16]{1,3,2,0:T(8,128)(2,1)S(1)}, u32[]{:S(2)}) copy-start(bf16[1,1024,4,16]{1,3,2,0:T(8,128)(2,1)S(1)} %get-tuple-element.273) | copy-start | bytes 393220
  147.8 39.6 %copy-start.80 = (f32[4,512]{1,0:T(4,128)}, f32[4,512]{1,0:T(4,128)S(1)}, u32[]{:S(2)}) copy-start(f32[4,512]{1,0:T(4,128)S(1)} %log_add_fusion.3) | copy-start | bytes 24580
  182.6 5.2 slice-start.1
  201.5 5.5 copy-start.19
  215.9 17.9 %copy-start.23 = (bf16[1,4,1024,64]{2,3,1,0:T(8,128)(2,1)}, bf16[1,4,1024,64]{2,3,1,0:T(8,128)(2,1)S(1)}, u32[]{:S(2)}) copy-start(bf16[1,4,1024,64]{2,3,1,0:T(8,128)(2,1)S(1)} %maximum_convert_fusion.2) | copy-start | bytes 1572868
  215.9 17.9 %copy-start.25 = (bf16[1,4,1024,64]{2,3,1,0:T(8,128)(2,1)}, bf16[1,4,1024,64]{2,3,1,0:T(8,128)(2,1)S(1)}, u32[]{:S(2)}) copy-start(bf16[1,4,1024,64]{2,3,1,0:T(8,128)(2,1)S(1)} %maximum_convert_fusion.3) | copy-start | bytes 1572868
  226.3 5.7 copy-start.43
  233.8 7.0 slice-start.8
  234.4 6.4 slice-start.9
  251.6 258.2 %reduce-scatter.29.cloned.1.call-start = ((), (), s32[]{:S(2)}) async-start(), calls=%async_computation.28 | async-start | bytes 4718592 | tf_op jit(solution)/shard_map/reduce_scatter | solution.py:263
  349.6 23.9 %copy-start.41 = (bf16[1,1024,1024]{2,1,0:T(8,128)(2,1)S(1)}, bf16[1,1024,1024]{2,1,0:T(8,128)(2,1)}, u32[]{:S(2)}) copy-start(bf16[1,1024,1024]{2,1,0:T(8,128)(2,1)} %all-gather.26.cloned.1.call-done) | copy-start | bytes 6291460
  381.2 169.8 %reduce-scatter.15.cloned.1.call-start = ((), (), s32[]{:S(2)}) async-start(), calls=%async_computation.20 | async-start | bytes 5242880 | tf_op jit(solution)/shard_map/reduce_scatter | solution.py:248
  381.3 7.1 copy-start.8
  381.3 7.1 copy-start.66
  381.3 7.1 copy-start.84
  385.4 9.6 slice-start.6
  388.4 6.6 slice-start.7
  408.1 5.0 copy-start.50
  413.1 217.5 %reduce-scatter.19.cloned.1.call-start = ((), (), s32[]{:S(2)}) async-start(), calls=%async_computation.23 | async-start | bytes 5242880 | tf_op jit(solution)/shard_map/reduce_scatter | solution.py:248
  429.4 280.8 %reduce-scatter.21.cloned.1.call-start = ((), (), s32[]{:S(2)}) async-start(), calls=%async_computation.24 | async-start | bytes 5242880 | tf_op jit(solution)/shard_map/reduce_scatter | solution.py:249
  431.1 8.7 copy-start.109
  444.3 345.3 %reduce-scatter.17.cloned.1.call-start = ((), (), s32[]{:S(2)}) async-start(), calls=%async_computation.21 | async-start | bytes 5242880 | tf_op jit(solution)/shard_map/reduce_scatter | solution.py:249
  445.9 8.3 copy-start.110
  458.7 5.5 copy-start.22
  458.7 5.5 copy-start.26
  458.7 411.6 %reduce-scatter.13.cloned.1.call-start = ((), (), s32[]{:S(2)}) async-start(), calls=%async_computation.18 | async-start | bytes 5242880 | tf_op jit(solution)/shard_map/reduce_scatter | solution.py:159
  467.0 482.6 %reduce-scatter.11.cloned.1.call-start = ((), (), s32[]{:S(2)}) async-start(), calls=%async_computation.15 | async-start | bytes 5242880 | tf_op jit(solution)/shard_map/reduce_scatter | solution.py:159
  473.9 526.7 %reduce-scatter.23.cloned.1.call-start = ((), (), s32[]{:S(2)}) async-start(), calls=%async_computation.25 | async-start | bytes 3538944 | tf_op jit(solution)/shard_map/reduce_scatter | solution.py:260
  482.5 573.3 %reduce-scatter.27.cloned.1.call-start = ((), (), s32[]{:S(2)}) async-start(), calls=%async_computation.27 | async-start | bytes 4718592 | tf_op jit(solution)/shard_map/reduce_scatter | solution.py:262
  492.0 138.7 %copy-start.4 = (bf16[2,256,1024]{2,1,0:T(8,128)(2,1)S(1)}, bf16[2,256,1024]{2,1,0:T(8,128)(2,1)}, u32[]{:S(2)}) copy-start(bf16[2,256,1024]{2,1,0:T(8,128)(2,1)} %param.40) | copy-start | bytes 3145732
  492.0 138.7 %copy-start.83 = (f32[1024]{0:T(1024)S(1)}, f32[1024]{0:T(1024)}, u32[]{:S(2)}) copy-start(f32[1024]{0:T(1024)} %param.44) | copy-start | bytes 12292
  492.0 138.7 %copy-start.91 = (f32[256]{0:T(256)S(1)}, f32[256]{0:T(256)}, u32[]{:S(2)}) copy-start(f32[256]{0:T(256)} %copy-done.90) | copy-start | bytes 3076
  492.0 138.7 %copy-start.93 = (f32[256]{0:T(256)S(1)}, f32[256]{0:T(256)}, u32[]{:S(2)}) copy-start(f32[256]{0:T(256)} %copy-done.92) | copy-start | bytes 3076
  492.0 140.7 %copy-start.101 = (f32[256]{0:T(256)S(1)}, f32[256]{0:T(256)}, u32[]{:S(2)}) copy-start(f32[256]{0:T(256)} %copy-done.100) | copy-start | bytes 3076
  492.0 140.7 %copy-start.99 = (f32[256]{0:T(256)S(1)}, f32[256]{0:T(256)}, u32[]{:S(2)}) copy-start(f32[256]{0:T(256)} %copy-done.98) | copy-start | bytes 3076
  492.0 297.6 %copy-start.82 = (f32[1024]{0:T(1024)S(1)}, f32[1024]{0:T(1024)}, u32[]{:S(2)}) copy-start(f32[1024]{0:T(1024)} %param.46) | copy-start | bytes 12292
  492.0 297.6 %copy-start.95 = (f32[256]{0:T(256)S(1)}, f32[256]{0:T(256)}, u32[]{:S(2)}) copy-start(f32[256]{0:T(256)} %copy-done.94) | copy-start | bytes 3076
  492.0 297.6 %copy-start.97 = (f32[256]{0:T(256)S(1)}, f32[256]{0:T(256)}, u32[]{:S(2)}) copy-start(f32[256]{0:T(256)} %copy-done.96) | copy-start | bytes 3076
  710.2 82.8 %copy-start.14 = (f32[1,256,1024]{2,1,0:T(8,128)S(1)}, f32[1,256,1024]{2,1,0:T(8,128)}, u32[]{:S(2)}) copy-start(f32[1,256,1024]{2,1,0:T(8,128)} %reduce-scatter.21.cloned.1.call-done) | copy-start | bytes 3145732
  792.9 156.7 %copy-start.13 = (f32[1,256,1024]{2,1,0:T(8,128)S(1)}, f32[1,256,1024]{2,1,0:T(8,128)}, u32[]{:S(2)}) copy-start(f32[1,256,1024]{2,1,0:T(8,128)} %reduce-scatter.19.cloned.1.call-done) | copy-start | bytes 3145732
  792.9 156.7 %copy-start.102 = (f32[1024]{0:T(1024)S(1)}, f32[1024]{0:T(1024)}, u32[]{:S(2)}) copy-start(f32[1024]{0:T(1024)} %param.55) | copy-start | bytes 12292
  792.9 156.7 %copy-start.103 = (f32[1024]{0:T(1024)S(1)}, f32[1024]{0:T(1024)}, u32[]{:S(2)}) copy-start(f32[1024]{0:T(1024)} %param.51) | copy-start | bytes 12292
  839.7 216.1 %copy-start.104 = (f32[1024]{0:T(1024)}, f32[1024]{0:T(1024)S(1)}, u32[]{:S(2)}) copy-start(f32[1024]{0:T(1024)S(1)} %get-tuple-element.342) | copy-start | bytes 12292
  (87 other events, 239.8 us)
Sparse Core Ops, SparseCore 0:
  9.9 29.7 all-gather.11
  41.9 45.9 all-gather.9
  89.4 44.6 all-gather.19
  135.5 44.6 all-gather.23
  181.6 44.6 all-gather.25
  228.3 44.6 all-gather.21
  274.9 26.5 all-gather.15
  303.7 45.9 all-gather.13
  351.5 26.6 all-gather.17
  381.2 36.0 reduce-scatter.24
  420.7 51.3 reduce-scatter.28
  474.3 76.7 reduce-scatter.14
  553.4 77.2 reduce-scatter.18
  632.9 77.2 reduce-scatter.20
  712.3 77.2 reduce-scatter.16
  791.9 78.3 reduce-scatter.12
  872.4 77.2 reduce-scatter.10
  953.8 46.7 reduce-scatter.22
  1004.5 51.2 reduce-scatter.26
where the time goes:
time: 1070 us; the launch traced here: 1060 us
  waiting for transfers between devices  709 us (66%)
  matrix products  181 us (17%)
  blocking collectives  72.7 us (7%)
  other arithmetic  48.3 us (5%)
  local copies, waits for them, and re-layouts  35.3 us (3%)
  between operations  16.4 us (2%)
    reduce_scatter x2, waiting for transfers between devices, on_device(): lax.psum_scatter(grad_two, 'tensor', scatter_dimension=1, tiled=True)  157 us
    reduce_scatter x2, waiting for transfers between devices, on_device(): lax.psum_scatter(grad_one, 'tensor', scatter_dimension=1, tiled=True)  119 us
    reduce_scatter x2, waiting for transfers between devices, on_device(): lax.psum_scatter(partial_sum, 'tensor', scatter_dimension=1, tiled=True)  110 us
    all_gather x2, waiting for transfers between devices, on_device(): lax.all_gather(value_one.astype(jnp.bfloat16), 'tensor', axis=1, tiled=True)  85.3 us
    all_gather x2, waiting for transfers between devices, on_device(): lax.all_gather(value_two.astype(jnp.bfloat16), 'tensor', axis=1, tiled=True)  62.8 us
    reduce_scatter x1, waiting for transfers between devices, on_device(): lax.psum_scatter(grad_upw, 'dp', scatter_dimension=0, tiled=True)  55.3 us
    reduce_scatter x1, waiting for transfers between devices, on_device(): lax.psum_scatter(grad_qkv, 'dp', scatter_dimension=0, tiled=True)  45.7 us
    psum x1, blocking collectives, on_device(): lax.psum((sum_gain_one, sum_bias_one, sum_gain_two, sum_bias_two, sum_slo...  44 us
  transfers between devices with their start and end apart: 19, of which 16 were waited for; matrix products, arithmetic and copies ran while one was open for 23% of the time, Pallas kernels for 0%

commit v1 on v0

--- a/solution.py
+++ b/solution.py
@@ -7,6 +7,18 @@
 ROT = 16
 BLOCK = 256
 MICRO = 2
+
+
+def gather_by_bits(x, axis, dim):
+    ways, here = (lax.axis_size(axis), lax.axis_index(axis))
+    grown, reach = (x, 1)
+    while reach < ways:
+        theirs = lax.ppermute(grown, axis, [(d, d ^ reach) for d in range(ways)])
+        mine_first = jnp.concatenate([grown, theirs], axis=dim)
+        theirs_first = jnp.concatenate([theirs, grown], axis=dim)
+        grown = jnp.where(here & reach == 0, mine_first, theirs_first)
+        reach = 2 * reach
+    return grown
 
 
 def layer_norm(values, ln_gain, ln_bias):
@@ -100,7 +112,7 @@
         qkv_full, out_full, up_full, down_full = (
             lax.all_gather(w_qkv, "dp", axis=0, tiled=True),
             lax.all_gather(w_out, "dp", axis=0, tiled=True),
-            lax.all_gather(w_up, "dp", axis=0, tiled=True),
+            gather_by_bits(w_up, "dp", 0),
             lax.all_gather(w_down, "dp", axis=0, tiled=True),
         )
         projected = (

time: 1070 us -> 1070 us (level)
  waiting for transfers between devices: 709 us -> 692 us
    all_gather x1, waiting for transfers between devices: 28.5 us -> 0.01 us  [on_device(): lax.all_gather(w_up, 'dp', axis=0, tiled=True)]
    reduce_scatter x2, waiting for transfers between devices: 119 us -> 143 us  [on_device(): lax.psum_scatter(grad_one, 'tensor', scatter_dimension=1, tiled=True)]
    all_gather x2, waiting for transfers between devices: 85.3 us -> 70.2 us  [on_device(): lax.all_gather(value_one.astype(jnp.bfloat16), 'tensor', axis=1, tiled=True)]
    ppermute x0 -> x3, waiting for transfers between devices: none -> 10.9 us  [gather_by_bits(): theirs = lax.ppermute(grown, axis, [(d, d ^ reach) for d in range(ways)])]
    unnamed x267 -> x291, local copies, waits for them, and re-layouts: 23.3 us -> 26.5 us
  transfers between devices with their start and end apart: 19 -> 22, of which waited for: 16 -> 15; matrix products, arithmetic and copies ran while one was open for 23% -> 24% of each run, Pallas kernels for 0% -> 0%
where the time goes in v1:
time: 1070 us; the launch traced here: 1060 us
  waiting for transfers between devices  692 us (65%)
  matrix products  189 us (18%)
  blocking collectives  71.5 us (7%)
  other arithmetic  52.7 us (5%)
  local copies, waits for them, and re-layouts  36 us (3%)
  between operations  16.6 us (2%)
    reduce_scatter x2, waiting for transfers between devices, on_device(): lax.psum_scatter(grad_two, 'tensor', scatter_dimension=1, tiled=True)  157 us
    reduce_scatter x2, waiting for transfers between devices, on_device(): lax.psum_scatter(grad_one, 'tensor', scatter_dimension=1, tiled=True)  143 us
    reduce_scatter x2, waiting for transfers between devices, on_device(): lax.psum_scatter(partial_sum, 'tensor', scatter_dimension=1, tiled=True)  110 us
    all_gather x2, waiting for transfers between devices, on_device(): lax.all_gather(value_one.astype(jnp.bfloat16), 'tensor', axis=1, tiled=True)  70.2 us
    reduce_scatter x1, waiting for transfers between devices, on_device(): lax.psum_scatter(grad_upw, 'dp', scatter_dimension=0, tiled=True)  55.3 us
    all_gather x2, waiting for transfers between devices, on_device(): lax.all_gather(value_two.astype(jnp.bfloat16), 'tensor', axis=1, tiled=True)  54.4 us
    reduce_scatter x1, waiting for transfers between devices, on_device(): lax.psum_scatter(grad_qkv, 'dp', scatter_dimension=0, tiled=True)  45.7 us
    psum x1, blocking collectives, on_device(): lax.psum((sum_gain_one, sum_bias_one, sum_gain_two, sum_bias_two, sum_slo...  43.9 us
  transfers between devices with their start and end apart: 22, of which 15 were waited for; matrix products, arithmetic and copies ran while one was open for 24% of the time, Pallas kernels for 0%

profile of v1, /device:TPU:0, one launch (start us, length us, event | category | flops | bytes accessed | tf_op | source)
XLA Modules:
  0.0 1062.8 jit_solution(9862540360306366833)
XLA Ops:
  11.7 3.2 fusion.173
  23.1 12.5 %all_gather.42 = bf16[1024,256]{1,0:T(8,128)(2,1)S(1)} all-gather(bf16[128,256]{1,0:T(8,128)(2,1)S(1)} %copy-done.93), channel_id=1, replica_groups=mesh['dp'=8,'tensor'=4] {'dp'}, dimensions={0}, use_global_device_ids=true | all-gather | bytes 589824 | tf_op jit(solution)/shard_map/all_gather | solution.py:114
  40.2 10.9 %collective-permute-done.1 = bf16[256,1024]{1,0:T(8,128)(2,1)S(1)} collective-permute-done((bf16[256,1024]{1,0:T(8,128)(2,1)S(1)}, bf16[256,1024]{1,0:T(8,128)(2,1)S(1)}, u32[]{:S(2)}, u32[]{:S(2)}) %collective-permute-start.1) | collective-permute-done | bytes 524320 | tf_op jit(solution)/shard_map/ppermute | solution.py:16
  54.1 33.0 %all-gather.10.cloned.1.call-done = bf16[1,1024,1024]{2,1,0:T(8,128)(2,1)} async-done(((bf16[1,256,1024]{2,1,0:T(8,128)(2,1)}), bf16[1,1024,1024]{2,1,0:T(8,128)(2,1)}) %all-gather.10.cloned.1.call-update) | async-done | bytes 2097168 | tf_op jit(solution)/shard_map/all_gather | solution.py:109
  87.2 3.9 fusion.85
  96.3 37.2 %all-gather.18.cloned.1.call-done = bf16[1,1024,1024]{2,1,0:T(8,128)(2,1)} async-done(((bf16[1,256,1024]{2,1,0:T(8,128)(2,1)}), bf16[1,1024,1024]{2,1,0:T(8,128)(2,1)}) %all-gather.18.cloned.1.call-update) | async-done | bytes 2097168 | tf_op jit(solution)/shard_map/all_gather | solution.py:109
  133.4 3.9 fusion.91
  144.1 2.8 fusion.161
  148.5 2.3 fusion
  151.8 4.5 fusion.155
  158.0 2.6 fusion.1
  161.4 3.1 fusion.154
  168.4 2.8 fusion.160
  171.1 8.4 all-gather.22.cloned.1.call-done
  179.5 2.3 fusion.142
  181.9 4.7 multiply_reduce_fusion.3
  192.5 33.1 %all-gather.26.cloned.1.call-done = bf16[1,1024,1024]{2,1,0:T(8,128)(2,1)} async-done(((bf16[1,256,1024]{2,1,0:T(8,128)(2,1)}), bf16[1,1024,1024]{2,1,0:T(8,128)(2,1)}) %all-gather.26.cloned.1.call-update) | async-done | bytes 2097168 | tf_op jit(solution)/shard_map/all_gather | solution.py:174
  225.6 2.4 fusion.46
  229.8 6.9 multiply_reduce_fusion.1
  236.7 4.6 multiply_convert_fusion.1
  243.3 2.2 fusion.158
  245.6 2.5 fusion.145
  248.2 4.3 fusion.122
  252.5 4.8 multiply_reduce_fusion.2
  257.4 15.0 %all-gather.20.cloned.1.call-done = bf16[1,1024,1024]{2,1,0:T(8,128)(2,1)} async-done(((bf16[1,256,1024]{2,1,0:T(8,128)(2,1)}), bf16[1,1024,1024]{2,1,0:T(8,128)(2,1)}) %all-gather.20.cloned.1.call-update) | async-done | bytes 2097168 | tf_op jit(solution)/shard_map/all_gather | solution.py:110
  272.3 7.4 fusion.66
  279.7 39.4 %all-gather.14.cloned.1.call-done = bf16[1,1024,1024]{2,1,0:T(8,128)(2,1)} async-done(((bf16[1,256,1024]{2,1,0:T(8,128)(2,1)}), bf16[1,1024,1024]{2,1,0:T(8,128)(2,1)}) %all-gather.14.cloned.1.call-update) | async-done | bytes 2097168 | tf_op jit(solution)/shard_map/all_gather | solution.py:110
  319.1 24.1 %multiply_convert_fusion.5 = (bf16[1024,1024]{1,0:T(8,128)(2,1)S(1)}, f32[1024,1024]{1,0:T(8,128)}, bf16[1024,1024]{1,0:T(8,128)(2,1)S(1)}, f32[1024,1024]{1,0:T(8,128)}, f32[1024,1024]{1,0:T(8,128)}) fusion(f32[1024]{0:T(1024)S(1)} %copy-done.126, f32[1024,1024]{1,0:T(8,128)} %fusion.66, bf16[512,1024]{1,0:T(8,128)(2,1)} %collective-permute-done.2, ...), kind=kOutput, calls=%fused_computation.58 | convolution fusion | flops 2295332864 | bytes 25169920 | tf_op jit(solution)/shard_map/bsd,df->bsf/dot_general | solution.py:164
  343.4 2.4 fusion.44
  349.6 2.0 multiply_convert_fusion.2
  351.6 4.5 add_bitcast_fusion
  360.4 3.0 fusion.156
  363.4 5.9 multiply_reduce_fusion
  369.4 2.1 multiply_convert_fusion
  379.7 2.2 fusion.139
  383.4 3.9 convolution_bitcast_fusion.1
  388.9 4.5 fusion.151
  393.4 4.7 fusion.133
  399.7 3.9 convolution_bitcast_fusion
  405.2 7.7 convert_reduce_fusion
  412.9 6.6 convolution_bitcast_fusion.2
  421.1 6.8 convert_reduce_fusion.1
  429.3 4.4 convolution_bitcast_fusion.3
  435.4 4.0 fusion.254
  439.4 2.7 add_bitcast_fusion.1
  442.2 4.2 fusion.253
  446.4 2.8 add_bitcast_fusion.2
  450.6 3.7 fusion.68
  454.3 3.6 fusion.88
  458.0 4.8 fusion.64
  462.8 4.5 fusion.80
  468.1 15.1 %all-reduce.5 = (f32[768]{0:T(1024)}, f32[1024]{0:T(1024)}) all-reduce(f32[768]{0:T(1024)S(1)} %add.401, f32[1024]{0:T(1024)S(1)} %add.402), channel_id=1, replica_groups=mesh['dp'=8,'tensor'=4] {'dp'}, use_global_device_ids=true, to_apply=%region_36.37 | all-reduce | flops 1792 | bytes 14336 | tf_op jit(solution)/shard_map/psum | solution.py:277
  486.9 63.6 %reduce-scatter.15.cloned.1.call-done = f32[1,256,1024]{2,1,0:T(8,128)} async-done(((f32[1,1024,1024]{2,1,0:T(8,128)}), f32[1,256,1024]{2,1,0:T(8,128)}) %reduce-scatter.15.cloned.1.call-update) | async-done | bytes 1048592 | tf_op jit(solution)/shard_map/reduce_scatter | solution.py:260
  550.4 79.6 %reduce-scatter.19.cloned.1.call-done = f32[1,256,1024]{2,1,0:T(8,128)} async-done(((f32[1,1024,1024]{2,1,0:T(8,128)}), f32[1,256,1024]{2,1,0:T(8,128)}) %reduce-scatter.19.cloned.1.call-update) | async-done | bytes 1048592 | tf_op jit(solution)/shard_map/reduce_scatter | solution.py:260
  630.0 2.0 fusion.177
  632.1 77.5 %reduce-scatter.21.cloned.1.call-done = f32[1,256,1024]{2,1,0:T(8,128)} async-done(((f32[1,1024,1024]{2,1,0:T(8,128)}), f32[1,256,1024]{2,1,0:T(8,128)}) %reduce-scatter.21.cloned.1.call-update) | async-done | bytes 1048592 | tf_op jit(solution)/shard_map/reduce_scatter | solution.py:261
  709.6 79.4 %reduce-scatter.17.cloned.1.call-done = f32[1,256,1024]{2,1,0:T(8,128)} async-done(((f32[1,1024,1024]{2,1,0:T(8,128)}), f32[1,256,1024]{2,1,0:T(8,128)}) %reduce-scatter.17.cloned.1.call-update) | async-done | bytes 1048592 | tf_op jit(solution)/shard_map/reduce_scatter | solution.py:261
  789.0 3.2 fusion.178
  795.1 43.9 %all-reduce.4 = (f32[1024]{0:T(1024)}, f32[1024]{0:T(1024)}, f32[1024]{0:T(1024)}, f32[1024]{0:T(1024)}, f32[1024]{0:T(1024)S(1)}) all-reduce(f32[1024]{0:T(1024)S(1)} %add.403, f32[1024]{0:T(1024)S(1)} %add.404, f32[1024]{0:T(1024)S(1)} %add.405, f32[1024]{0:T(1024)S(1)} %add.406, ...), channel_id=1, replica_groups=mesh['dp'=8,'tensor'=4] {'dp','tensor'}, use_global_device_ids=true, to_apply=%region_42.43 | all-reduce | flops 5120 | bytes 40960 | tf_op jit(solution)/shard_map/psum | solution.py:278
  839.1 30.5 %reduce-scatter.13.cloned.1.call-done = f32[1,256,1024]{2,1,0:T(8,128)} async-done(((f32[1,1024,1024]{2,1,0:T(8,128)}), f32[1,256,1024]{2,1,0:T(8,128)}) %reduce-scatter.13.cloned.1.call-update) | async-done | bytes 1048592 | tf_op jit(solution)/shard_map/reduce_scatter | solution.py:171
  869.6 79.4 %reduce-scatter.11.cloned.1.call-done = f32[1,256,1024]{2,1,0:T(8,128)} async-done(((f32[1,1024,1024]{2,1,0:T(8,128)}), f32[1,256,1024]{2,1,0:T(8,128)}) %reduce-scatter.11.cloned.1.call-update) | async-done | bytes 1048592 | tf_op jit(solution)/shard_map/reduce_scatter | solution.py:171
  949.0 2.7 fusion.181
  954.2 45.7 %reduce-scatter.23.cloned.1.call-done = f32[128,768]{1,0:T(8,128)} async-done(((f32[1024,768]{1,0:T(8,128)}), f32[128,768]{1,0:T(8,128)}) %reduce-scatter.23.cloned.1.call-update) | async-done | bytes 393232 | tf_op jit(solution)/shard_map/reduce_scatter | solution.py:272
  999.9 55.3 %reduce-scatter.27.cloned.1.call-done = f32[128,1024]{1,0:T(8,128)} async-done(((f32[1024,1024]{1,0:T(8,128)}), f32[128,1024]{1,0:T(8,128)}) %reduce-scatter.27.cloned.1.call-update) | async-done | bytes 524304 | tf_op jit(solution)/shard_map/reduce_scatter | solution.py:274
  (447 shorter events, 88.4 us)
Async XLA Ops:
  7.2 8.5 copy-start.18
  7.2 46.9 %all-gather.12.cloned.1.call-start = ((), (), s32[]{:S(2)}) async-start(), calls=%async_computation.11 | async-start | bytes 1769472 | tf_op jit(solution)/shard_map/all_gather | solution.py:113
  7.9 79.2 %all-gather.10.cloned.1.call-start = ((), (), s32[]{:S(2)}) async-start(), calls=%async_computation.10 | async-start | bytes 2621440 | tf_op jit(solution)/shard_map/all_gather | solution.py:109
  9.4 8.0 copy-start.97
  9.4 7.9 copy-start.95
  11.6 7.9 copy-start.67
  11.6 8.6 copy-start.118
  11.7 10.5 copy-start.94
  11.7 11.5 %copy-start.93 = (bf16[128,256]{1,0:T(8,128)(2,1)S(1)}, bf16[128,256]{1,0:T(8,128)(2,1)}, u32[]{:S(2)}) copy-start(bf16[128,256]{1,0:T(8,128)(2,1)} %param.50) | copy-start | bytes 196612
  14.9 21.8 %copy-start.68 = (bf16[128,1024]{1,0:T(8,128)(2,1)S(1)}, bf16[128,1024]{1,0:T(8,128)(2,1)}, u32[]{:S(2)}) copy-start(bf16[128,1024]{1,0:T(8,128)(2,1)} %param.52) | copy-start | bytes 786436
  14.9 118.5 %all-gather.18.cloned.1.call-start = ((), (), s32[]{:S(2)}) async-start(), calls=%async_computation.15 | async-start | bytes 2621440 | tf_op jit(solution)/shard_map/all_gather | solution.py:109
  15.6 163.9 %all-gather.22.cloned.1.call-start = ((), (), s32[]{:S(2)}) async-start(), calls=%async_computation.18 | async-start | bytes 2621440 | tf_op jit(solution)/shard_map/all_gather | solution.py:174
  16.7 70.4 %copy-start.125 = (f32[768]{0:T(1024)S(1)}, f32[768]{0:T(1024)}, u32[]{:S(2)}) copy-start(f32[768]{0:T(1024)} %param.49) | copy-start | bytes 9220
  16.8 208.9 %all-gather.26.cloned.1.call-start = ((), (), s32[]{:S(2)}) async-start(), calls=%async_computation.22 | async-start | bytes 2621440 | tf_op jit(solution)/shard_map/all_gather | solution.py:174
  17.4 254.9 %all-gather.20.cloned.1.call-start = ((), (), s32[]{:S(2)}) async-start(), calls=%async_computation.16 | async-start | bytes 2621440 | tf_op jit(solution)/shard_map/all_gather | solution.py:110
  17.9 301.2 %all-gather.14.cloned.1.call-start = ((), (), s32[]{:S(2)}) async-start(), calls=%async_computation.12 | async-start | bytes 2621440 | tf_op jit(solution)/shard_map/all_gather | solution.py:110
  18.7 385.0 %all-gather.16.cloned.1.call-start = ((), (), s32[]{:S(2)}) async-start(), calls=%async_computation.13 | async-start | bytes 2359296 | tf_op jit(solution)/shard_map/all_gather | solution.py:116
  19.5 393.5 %all-gather.24.cloned.1.call-start = ((), (), s32[]{:S(2)}) async-start(), calls=%async_computation.20 | async-start | bytes 2359296 | tf_op jit(solution)/shard_map/all_gather | solution.py:178
  19.5 17.2 %collective-permute-start = (bf16[128,1024]{1,0:T(8,128)(2,1)S(1)}, bf16[128,1024]{1,0:T(8,128)(2,1)S(1)}, u32[]{:S(2)}, u32[]{:S(2)}) collective-permute-start(bf16[128,1024]{1,0:T(8,128)(2,1)S(1)} %copy-done.67), channel_id=1, source_target_pairs={{0,4},{4,0},{8,12},{12,8},{16,20},{20,16},{24,28},{28,24},{1,5},{5... | collective-permute-start | bytes 786440 | tf_op jit(solution)/shard_map/ppermute | solution.py:16
  20.2 463.0 %reduce-scatter.25.cloned.1.call-start = ((), (), s32[]{:S(2)}) async-start(), calls=%async_computation.26 | async-start | bytes 1179648 | tf_op jit(solution)/shard_map/reduce_scatter | solution.py:273
  35.6 210.0 %copy-start.23 = (bf16[1024,256]{1,0:T(8,128)(2,1)}, bf16[1024,256]{1,0:T(8,128)(2,1)S(1)}, u32[]{:S(2)}) copy-start(bf16[1024,256]{1,0:T(8,128)(2,1)S(1)} %all_gather.42) | copy-start | bytes 1572868
  36.7 123.9 %copy-start.9 = (pred[512,1024]{1,0:T(8,128)(4,1)}, pred[512,1024]{1,0:T(8,128)(4,1)S(1)}, u32[]{:S(2)}) copy-start(pred[512,1024]{1,0:T(8,128)(4,1)S(1)} %compare_and_fusion) | copy-start | bytes 1572868
  36.9 14.2 %collective-permute-start.1 = (bf16[256,1024]{1,0:T(8,128)(2,1)S(1)}, bf16[256,1024]{1,0:T(8,128)(2,1)S(1)}, u32[]{:S(2)}, u32[]{:S(2)}) collective-permute-start(bf16[256,1024]{1,0:T(8,128)(2,1)S(1)} %maximum_select_fusion.2), channel_id=1, source_target_pairs={{0,8},{4,12},{8,0},{12,4},{16,24},{20,28},{24,16},{28,20},{1,9},{5... | collective-permute-start | bytes 1572872 | tf_op jit(solution)/shard_map/ppermute | solution.py:16
  39.6 197.1 %copy-start.12 = (pred[512,1024]{1,0:T(8,128)(4,1)}, pred[512,1024]{1,0:T(8,128)(4,1)S(1)}, u32[]{:S(2)}) copy-start(pred[512,1024]{1,0:T(8,128)(4,1)S(1)} %compare_and_fusion.1) | copy-start | bytes 1572868
  40.1 146.5 %copy-start.7 = (pred[512,768]{1,0:T(8,128)(4,1)}, pred[512,768]{1,0:T(8,128)(4,1)S(1)}, u32[]{:S(2)}) copy-start(pred[512,768]{1,0:T(8,128)(4,1)S(1)} %get-tuple-element.314) | copy-start | bytes 1179652
  52.6 204.8 %collective-permute-start.2 = (bf16[512,1024]{1,0:T(8,128)(2,1)}, bf16[512,1024]{1,0:T(8,128)(2,1)}, u32[]{:S(2)}, u32[]{:S(2)}) collective-permute-start(bf16[512,1024]{1,0:T(8,128)(2,1)} %maximum_select_fusion.1), channel_id=1, source_target_pairs={{0,16},{4,20},{8,24},{12,28},{16,0},{20,4},{24,8},{28,12},{1,17},{... | collective-permute-start | bytes 3145736 | tf_op jit(solution)/shard_map/ppermute | solution.py:16
  137.3 23.3 %copy-start.29 = (f32[1024,768]{0,1:T(8,128)}, f32[1024,768]{0,1:T(8,128)S(1)}, u32[]{:S(2)}) copy-start(f32[1024,768]{0,1:T(8,128)S(1)} %fusion.91) | copy-start | bytes 9437188
  137.4 30.0 %copy-start.49 = (bf16[1,4,1024,64]{2,3,1,0:T(8,128)(2,1)}, bf16[1,4,1024,64]{2,3,1,0:T(8,128)(2,1)S(1)}, u32[]{:S(2)}) copy-start(bf16[1,4,1024,64]{2,3,1,0:T(8,128)(2,1)S(1)} %fusion.240) | copy-start | bytes 1572868
  138.0 18.5 %copy-start.35 = (bf16[1,1024,4,48]{1,3,2,0:T(8,128)(2,1)}, bf16[1,1024,4,48]{1,3,2,0:T(8,128)(2,1)S(1)}, u32[]{:S(2)}) copy-start(bf16[1,1024,4,48]{1,3,2,0:T(8,128)(2,1)S(1)} %slice.684) | copy-start | bytes 1179652
  140.8 15.7 %copy-start.60 = (bf16[1,1024,4,16]{1,3,2,0:T(8,128)(2,1)}, bf16[1,1024,4,16]{1,3,2,0:T(8,128)(2,1)S(1)}, u32[]{:S(2)}) copy-start(bf16[1,1024,4,16]{1,3,2,0:T(8,128)(2,1)S(1)} %get-tuple-element.273) | copy-start | bytes 393220
  156.4 8.1 copy-start.21
  156.5 8.0 copy-start.39
  168.4 13.5 %copy-start.52 = (bf16[1,4,1024,64]{2,3,1,0:T(8,128)(2,1)S(1)}, bf16[1,4,1024,64]{2,3,1,0:T(8,128)(2,1)}, u32[]{:S(2)}) copy-start(bf16[1,4,1024,64]{2,3,1,0:T(8,128)(2,1)} %fusion.239) | copy-start | bytes 1572868
  188.9 39.2 %copy-start.25 = (bf16[1,4,1024,64]{2,3,1,0:T(8,128)(2,1)}, bf16[1,4,1024,64]{2,3,1,0:T(8,128)(2,1)S(1)}, u32[]{:S(2)}) copy-start(bf16[1,4,1024,64]{2,3,1,0:T(8,128)(2,1)S(1)} %maximum_convert_fusion.2) | copy-start | bytes 1572868
  189.0 39.1 %copy-start.27 = (bf16[1,4,1024,64]{2,3,1,0:T(8,128)(2,1)}, bf16[1,4,1024,64]{2,3,1,0:T(8,128)(2,1)S(1)}, u32[]{:S(2)}) copy-start(bf16[1,4,1024,64]{2,3,1,0:T(8,128)(2,1)S(1)} %maximum_convert_fusion.3) | copy-start | bytes 1572868
  189.0 47.7 %copy-start.85 = (f32[4,512]{1,0:T(4,128)}, f32[4,512]{1,0:T(4,128)S(1)}, u32[]{:S(2)}) copy-start(f32[4,512]{1,0:T(4,128)S(1)} %log_add_fusion.2) | copy-start | bytes 24580
  245.5 239.3 %reduce-scatter.29.cloned.1.call-start = ((), (), s32[]{:S(2)}) async-start(), calls=%async_computation.28 | async-start | bytes 4718592 | tf_op jit(solution)/shard_map/reduce_scatter | solution.py:275
  257.4 61.8 %copy-start.126 = (f32[1024]{0:T(1024)S(1)}, f32[1024]{0:T(1024)}, u32[]{:S(2)}) copy-start(f32[1024]{0:T(1024)} %param.53) | copy-start | bytes 12292
  279.7 63.6 %copy-start.43 = (bf16[1,1024,1024]{2,1,0:T(8,128)(2,1)S(1)}, bf16[1,1024,1024]{2,1,0:T(8,128)(2,1)}, u32[]{:S(2)}) copy-start(bf16[1,1024,1024]{2,1,0:T(8,128)(2,1)} %all-gather.26.cloned.1.call-done) | copy-start | bytes 6291460
  343.3 8.3 copy-start.128
  356.2 194.2 %reduce-scatter.15.cloned.1.call-start = ((), (), s32[]{:S(2)}) async-start(), calls=%async_computation.19 | async-start | bytes 5242880 | tf_op jit(solution)/shard_map/reduce_scatter | solution.py:260
  360.4 8.9 slice-start.8
  387.3 242.7 %reduce-scatter.19.cloned.1.call-start = ((), (), s32[]{:S(2)}) async-start(), calls=%async_computation.23 | async-start | bytes 5242880 | tf_op jit(solution)/shard_map/reduce_scatter | solution.py:260
  403.6 305.9 %reduce-scatter.21.cloned.1.call-start = ((), (), s32[]{:S(2)}) async-start(), calls=%async_computation.24 | async-start | bytes 5242880 | tf_op jit(solution)/shard_map/reduce_scatter | solution.py:261
  419.6 369.4 %reduce-scatter.17.cloned.1.call-start = ((), (), s32[]{:S(2)}) async-start(), calls=%async_computation.21 | async-start | bytes 5242880 | tf_op jit(solution)/shard_map/reduce_scatter | solution.py:261
  421.1 8.2 copy-start.122
  433.8 435.8 %reduce-scatter.13.cloned.1.call-start = ((), (), s32[]{:S(2)}) async-start(), calls=%async_computation.17 | async-start | bytes 5242880 | tf_op jit(solution)/shard_map/reduce_scatter | solution.py:171
  442.2 506.8 %reduce-scatter.11.cloned.1.call-start = ((), (), s32[]{:S(2)}) async-start(), calls=%async_computation.14 | async-start | bytes 5242880 | tf_op jit(solution)/shard_map/reduce_scatter | solution.py:171
  449.2 550.7 %reduce-scatter.23.cloned.1.call-start = ((), (), s32[]{:S(2)}) async-start(), calls=%async_computation.25 | async-start | bytes 3538944 | tf_op jit(solution)/shard_map/reduce_scatter | solution.py:272
  457.9 597.3 %reduce-scatter.27.cloned.1.call-start = ((), (), s32[]{:S(2)}) async-start(), calls=%async_computation.27 | async-start | bytes 4718592 | tf_op jit(solution)/shard_map/reduce_scatter | solution.py:274
  467.3 162.7 %copy-start.4 = (bf16[2,256,1024]{2,1,0:T(8,128)(2,1)S(1)}, bf16[2,256,1024]{2,1,0:T(8,128)(2,1)}, u32[]{:S(2)}) copy-start(bf16[2,256,1024]{2,1,0:T(8,128)(2,1)} %param.40) | copy-start | bytes 3145732
  467.3 162.7 %copy-start.84 = (f32[1024]{0:T(1024)S(1)}, f32[1024]{0:T(1024)}, u32[]{:S(2)}) copy-start(f32[1024]{0:T(1024)} %param.44) | copy-start | bytes 12292
  467.3 162.7 %copy-start.96 = (f32[256]{0:T(256)S(1)}, f32[256]{0:T(256)}, u32[]{:S(2)}) copy-start(f32[256]{0:T(256)} %copy-done.95) | copy-start | bytes 3076
  467.3 162.7 %copy-start.98 = (f32[256]{0:T(256)S(1)}, f32[256]{0:T(256)}, u32[]{:S(2)}) copy-start(f32[256]{0:T(256)} %copy-done.97) | copy-start | bytes 3076
  467.3 164.7 %copy-start.114 = (f32[256]{0:T(256)S(1)}, f32[256]{0:T(256)}, u32[]{:S(2)}) copy-start(f32[256]{0:T(256)} %copy-done.113) | copy-start | bytes 3076
  467.3 164.7 %copy-start.112 = (f32[256]{0:T(256)S(1)}, f32[256]{0:T(256)}, u32[]{:S(2)}) copy-start(f32[256]{0:T(256)} %copy-done.111) | copy-start | bytes 3076
  467.3 321.7 %copy-start.83 = (f32[1024]{0:T(1024)S(1)}, f32[1024]{0:T(1024)}, u32[]{:S(2)}) copy-start(f32[1024]{0:T(1024)} %param.46) | copy-start | bytes 12292
  467.3 321.6 %copy-start.107 = (f32[256]{0:T(256)S(1)}, f32[256]{0:T(256)}, u32[]{:S(2)}) copy-start(f32[256]{0:T(256)} %copy-done.106) | copy-start | bytes 3076
  467.4 321.6 %copy-start.109 = (f32[256]{0:T(256)S(1)}, f32[256]{0:T(256)}, u32[]{:S(2)}) copy-start(f32[256]{0:T(256)} %copy-done.108) | copy-start | bytes 3076
  709.6 82.8 %copy-start.16 = (f32[1,256,1024]{2,1,0:T(8,128)S(1)}, f32[1,256,1024]{2,1,0:T(8,128)}, u32[]{:S(2)}) copy-start(f32[1,256,1024]{2,1,0:T(8,128)} %reduce-scatter.21.cloned.1.call-done) | copy-start | bytes 3145732
  792.2 156.7 %copy-start.15 = (f32[1,256,1024]{2,1,0:T(8,128)S(1)}, f32[1,256,1024]{2,1,0:T(8,128)}, u32[]{:S(2)}) copy-start(f32[1,256,1024]{2,1,0:T(8,128)} %reduce-scatter.19.cloned.1.call-done) | copy-start | bytes 3145732
  792.3 156.7 %copy-start.115 = (f32[1024]{0:T(1024)S(1)}, f32[1024]{0:T(1024)}, u32[]{:S(2)}) copy-start(f32[1024]{0:T(1024)} %param.55) | copy-start | bytes 12292
  792.3 156.7 %copy-start.116 = (f32[1024]{0:T(1024)S(1)}, f32[1024]{0:T(1024)}, u32[]{:S(2)}) copy-start(f32[1024]{0:T(1024)} %param.51) | copy-start | bytes 12292
  839.1 216.1 %copy-start.117 = (f32[1024]{0:T(1024)}, f32[1024]{0:T(1024)S(1)}, u32[]{:S(2)}) copy-start(f32[1024]{0:T(1024)S(1)} %get-tuple-element.342) | copy-start | bytes 12292
  (102 other events, 326.0 us)
Sparse Core Ops, SparseCore 0:
  9.9 29.0 all-gather.11
  41.2 45.9 all-gather.9
  88.7 44.6 all-gather.17
  134.8 44.6 all-gather.21
  180.9 44.6 all-gather.25
  227.6 44.6 all-gather.19
  274.5 44.6 all-gather.13
  321.0 26.6 all-gather.15
  349.6 27.8 all-gather.23
  380.5 36.0 reduce-scatter.24
  420.0 51.2 reduce-scatter.28
  473.6 76.7 reduce-scatter.14
  552.7 77.2 reduce-scatter.18
  632.2 77.2 reduce-scatter.20
  711.7 77.2 reduce-scatter.16
  791.2 78.3 reduce-scatter.12
  871.7 77.1 reduce-scatter.10
  953.1 46.7 reduce-scatter.22
  1003.8 51.3 reduce-scatter.26
